TPU v7x, 256 devices: a whole 4x4x8 slice. The times are simulated.
256 devices in a mesh: px: 32 (over z, x), py: 8 (over y, core).
Axes of the slice: x: 4, y: 4, z: 8, core: 2. Of those that a mesh axis runs over, the one named last changes fastest.
Arguments:
- counts: int32 [32], replicated, may hold values from 1 to 6, 64 in all
- coefficient: float32 [192, 8, 4096], P('px', 'py'), may hold values from 0.2 to 5
- signs: int32 [192, 8, 4096], P('px', 'py'), may hold values from 0 to 1
- basis_old: float32 [192, 8, 16, 4096], P('px', 'py'), may hold values from -8 to 8
- basis_last: float32 [192, 8, 16, 4096], P('px', 'py'), may hold values from -8 to 8
- residual_factor: float32 [16, 16], replicated, may hold values from -12 to 12
- previous_coef: float32 [32, 16], replicated, may hold values from -12 to 12
- sample_rows: int32 [2048], replicated, may hold values from 0 to 2097151, as said below
Outputs:
- new_block: float32 [192, 8, 16, 4096], P('px', 'py')
- sketch: float32 [48, 2048], P(None, ('px', 'py'))
- solution: float32 [32, 16], replicated
Inputs may be any that keep to these rules, and one draw needn't show every extreme that they name: Index i of px owns counts[i] consecutive patch columns, in px order; the largest count is exactly 6. `sample_rows`: distinct cell numbers, among them 0 and 2097151.
All inputs are finite; a program needn't handle non-finite values.
Results may differ from a plain program's by a relative error of at most 0.0003.
Values sent between devices are 32-bit elements; how exact they have to be, the bound alone decides.
No kernel may reach another device: no remote copies, remote signals or barrier semaphores. Data moves between devices by JAX's collectives and lax.ppermute only.
A program may use at most 256 MiB of HBM per device.

v0:
```python
import math
import jax
import jax.numpy as jnp
from jax import lax
from jax.sharding import PartitionSpec as P

PS = 16
K = 2048
MEANX = 2
CAP = 6
CELLS = 4096
highest = lax.Precision.HIGHEST


def extended(block, sides, width):
    for axis, dim in sides:
        count = lax.axis_size(axis)
        forward = [(i, i + 1) for i in range(count - 1)]
        backward = [(target, source) for source, target in forward]
        low = lax.ppermute(
            lax.slice_in_dim(block, block.shape[dim] - width, None, axis=dim), axis, forward
        )
        high = lax.ppermute(lax.slice_in_dim(block, 0, width, axis=dim), axis, backward)
        block = jnp.concatenate([low, block, high], axis=dim)
    return block


def parity_of(values):
    folded = values
    for amount in (16, 8, 4, 2, 1):
        folded = jnp.bitwise_xor(folded, jnp.right_shift(folded, amount))
    return jnp.bitwise_and(folded, 1)


def sign_table(length):
    indices = jnp.arange(length, dtype=jnp.int32)
    parity = parity_of(jnp.bitwise_and(indices[:, None], indices[None, :]))
    return (1 - 2 * parity).astype(jnp.float32)


def transform_cells(values):
    inner_len = min(CELLS, 128)
    outer_len = CELLS // inner_len
    shaped = values.reshape(values.shape[:-1] + (outer_len, inner_len))
    shaped = jnp.einsum("sjab,bd->sjad", shaped, sign_table(inner_len), precision=highest)
    shaped = jnp.einsum("ca,sjad->sjcd", sign_table(outer_len), shaped, precision=highest)
    return shaped.reshape(values.shape)


def shift_pair(cube_vals, low_plane, high_plane, axis_pos):
    below = jnp.concatenate(
        [
            jnp.expand_dims(low_plane, axis_pos),
            lax.slice_in_dim(cube_vals, 0, PS - 1, axis=axis_pos),
        ],
        axis=axis_pos,
    )
    above = jnp.concatenate(
        [lax.slice_in_dim(cube_vals, 1, PS, axis=axis_pos), jnp.expand_dims(high_plane, axis_pos)],
        axis=axis_pos,
    )
    return (below, above)


def apply_operator(last_local, kappa_local, held_count, slot_ids):
    channels = last_local.shape[1] + 1
    plane_size = PS * PS
    joined = jnp.concatenate([last_local, kappa_local[:, None]], axis=1)
    cube_vals = joined.reshape(CAP, channels, PS, PS, PS)
    first_face = cube_vals[0, :, 0].reshape(channels, plane_size)
    last_slot = lax.dynamic_index_in_dim(cube_vals, held_count - 1, 0, keepdims=False)
    last_face = last_slot[:, PS - 1].reshape(channels, plane_size)
    x_ghost = extended(jnp.stack([first_face, last_face]), (("px", 0),), 1)
    y_planes = jnp.stack([cube_vals[:, :, :, 0], cube_vals[:, :, :, PS - 1]]).reshape(
        2, CAP, channels, plane_size
    )
    y_ghost = extended(y_planes, (("py", 0),), 1)
    ghost_low = x_ghost[0].reshape(channels, PS, PS)
    ghost_high = x_ghost[3].reshape(channels, PS, PS)
    x_low = jnp.concatenate([ghost_low[None], cube_vals[:-1, :, PS - 1]], axis=0)
    next_faces = jnp.concatenate([cube_vals[1:, :, 0], jnp.zeros_like(cube_vals[:1, :, 0])], axis=0)
    x_high = jnp.where(
        (slot_ids == held_count - 1)[:, None, None, None], ghost_high[None], next_faces
    )
    y_low = y_ghost[0].reshape(CAP, channels, PS, PS)
    y_high = y_ghost[3].reshape(CAP, channels, PS, PS)
    z_zero = jnp.zeros((CAP, channels, PS, PS), jnp.float32)
    centre_vals = cube_vals[:, :-1]
    centre_kappa = cube_vals[:, -1:]
    diag_sum = jnp.zeros_like(centre_kappa)
    weighted = jnp.zeros_like(centre_vals)
    for low_plane, high_plane, axis_pos in (
        (x_low, x_high, 2),
        (y_low, y_high, 3),
        (z_zero, z_zero, 4),
    ):
        kappa_pair = shift_pair(centre_kappa, low_plane[:, -1:], high_plane[:, -1:], axis_pos)
        value_pair = shift_pair(centre_vals, low_plane[:, :-1], high_plane[:, :-1], axis_pos)
        for near_kappa, near_vals in zip(kappa_pair, value_pair):
            weight = 0.5 * (centre_kappa + near_kappa)
            diag_sum = diag_sum + weight
            weighted = weighted + weight * near_vals
    summed = diag_sum * centre_vals - weighted
    return summed.reshape(CAP, channels - 1, CELLS)


def normal_parts(sketch_cols, proj_coef, previous_coef, residual_factor):
    pair_count = proj_coef.shape[0]
    width_rhs = proj_coef.shape[1]
    pair_rows = sketch_cols[:pair_count]
    first_image = jnp.einsum("ab,ak->bk", previous_coef, pair_rows, precision=highest)
    second_image = (
        jnp.einsum("ab,ak->bk", proj_coef, pair_rows, precision=highest) + sketch_cols[pair_count:]
    )
    images = jnp.concatenate([first_image, second_image], axis=0)
    target = jnp.einsum("ab,ak->bk", residual_factor, sketch_cols[:width_rhs], precision=highest)
    return (
        jnp.dot(images, images.T, precision=highest),
        jnp.dot(images, target.T, precision=highest),
    )


def solve_normal(normal_gram, normal_cross):
    factor_low = jnp.linalg.cholesky(normal_gram)
    middle = lax.linalg.triangular_solve(factor_low, normal_cross, left_side=True, lower=True)
    return lax.linalg.triangular_solve(
        factor_low, middle, left_side=True, lower=True, transpose_a=True
    )


def body(
    counts, coefficient, signs, basis_old, basis_last, residual_factor, previous_coef, sample_rows
):
    px_index = lax.axis_index("px")
    py_index = lax.axis_index("py")
    py_count = lax.axis_size("py")
    device_count = lax.axis_size("px") * py_count
    total_cells = MEANX * device_count * CELLS
    offsets = jnp.cumsum(counts) - counts
    held_count = counts[px_index]
    slot_ids = jnp.arange(CAP, dtype=jnp.int32)
    live_weight = (slot_ids < held_count).astype(jnp.float32)
    old_local = basis_old[:, 0] * live_weight[:, None, None]
    last_local = basis_last[:, 0] * live_weight[:, None, None]
    image = (
        apply_operator(last_local, coefficient[:, 0], held_count, slot_ids)
        * live_weight[:, None, None]
    )
    pair = jnp.concatenate([old_local, last_local], axis=1)
    local_gram = jnp.einsum("sac,sbc->ab", pair, image, precision=highest)
    patch_ids = (offsets[px_index] + slot_ids) * py_count + py_index
    sign_flips = (1 - 2 * signs[:, 0]).astype(jnp.float32)
    share_width = K // device_count
    share_start = (px_index * py_count + py_index) * share_width
    proj_coef = lax.psum(local_gram, ("px", "py")) / total_cells
    new_local = image - jnp.einsum("sac,ab->sbc", pair, proj_coef, precision=highest)
    spread = transform_cells(jnp.concatenate([pair, new_local], axis=1) * sign_flips[:, None, :])
    picked = jnp.take(spread, sample_rows % CELLS, axis=2)
    parity = parity_of(jnp.bitwise_and(patch_ids[:, None], (sample_rows // CELLS)[None, :]))
    weights = (1 - 2 * parity).astype(jnp.float32) * live_weight[:, None]
    partial_value = jnp.einsum("sk,sjk->jk", weights, picked, precision=highest) * (
        1.0 / math.sqrt(total_cells)
    )
    sketch_whole = lax.psum(partial_value, ("px", "py"))
    sketch_mine = lax.dynamic_slice_in_dim(sketch_whole, share_start, share_width, 1)
    normal_gram, normal_cross = normal_parts(
        sketch_whole, proj_coef, previous_coef, residual_factor
    )
    solution = solve_normal(normal_gram, normal_cross)
    return (new_local[:, None], sketch_mine, solution)


def solution(mesh):
    in_specs = (
        P(),
        P("px", "py", None),
        P("px", "py", None),
        P("px", "py", None, None),
        P("px", "py", None, None),
        P(),
        P(),
        P(),
    )
    out_specs = (P("px", "py", None, None), P(None, ("px", "py")), P())
    return jax.shard_map(body, mesh=mesh, in_specs=in_specs, out_specs=out_specs, check_vma=False)
```

profile of v0, /device:TPU:1, one launch (start us, length us, event | category | flops | bytes accessed | tf_op | source)
XLA Modules:
  0.0 603.8 jit_solution(3196232569332509484)
XLA Ops:
  14.0 8.6 %reshape.92 = f32[6,17,16,16,16]{4,3,2,0,1:T(8,128)} reshape(f32[6,17,4096]{2,0,1:T(8,128)} %copy.21) | data formatting | bytes 3342336 | tf_op jit(solution)/shard_map/reshape | solution.py:69
  26.3 3.2 constant_dynamic-slice_fusion.1
  29.5 3.9 copy.22
  34.3 5.2 collective-permute-start
  39.5 10.8 %slice_reduce_fusion = (f32[6,17,16,16]{3,2,0,1:T(8,128)}, f32[6,17,16,16]{3,2,0,1:T(8,128)}) fusion(f32[6,17,16,16,16]{4,3,2,0,1:T(8,128)} %reshape.92), kind=kLoop, calls=%fused_computation.34 | loop fusion | bytes 417792 | tf_op jit(solution)/shard_map/slice | solution.py:74
  52.5 4.6 collective-permute-start.2
  59.3 3.0 collective-permute-start.3
  62.4 17.5 %fusion.102 = (f32[6,16,15,16,16]{4,3,2,0,1:T(8,128)}, f32[6,16,15,16,16]{4,3,2,0,1:T(8,128)}) fusion(f32[6,17,16,16,16]{4,3,2,0,1:T(8,128)} %reshape.92), kind=kLoop, calls=%fused_computation.173 | loop fusion | bytes 5898240 | tf_op jit(solution)/shard_map/slice | solution.py:59
  81.1 9.2 %fusion.101 = (f32[6,16,16,15,16]{4,3,2,0,1:T(8,128)}, f32[6,16,16,15,16]{4,3,2,0,1:T(8,128)}) fusion(f32[6,17,16,16,16]{4,3,2,0,1:T(8,128)S(1)} %bitcast.139), kind=kLoop, calls=%fused_computation.172 | loop fusion | bytes 5898240 | tf_op jit(solution)/shard_map/slice | solution.py:59
  90.3 9.8 %fusion.100 = (f32[6,16,16,16,15]{4,3,2,0,1:T(8,128)}, f32[6,16,16,16,15]{4,3,2,0,1:T(8,128)}) fusion(f32[6,17,16,16,16]{4,3,2,0,1:T(8,128)S(1)} %bitcast.139), kind=kLoop, calls=%fused_computation.171 | loop fusion | bytes 5898240 | tf_op jit(solution)/shard_map/slice | solution.py:54
  109.1 4.0 bitcast_multiply_fusion.1
  118.9 3.5 fusion.30
  134.3 5.0 add_bitcast_fusion
  139.3 37.8 %fusion = f32[6,16,16,16,16]{4,3,2,0,1:T(8,128)} fusion(f32[6,17,16,16,16]{4,3,2,0,1:T(8,128)} %reshape.92, f32[6,16,15,16,16]{4,3,2,0,1:T(8,128)} %get-tuple-element.29, f32[6,16,1,16,16]{4,3,2,0,1:T(8,128)} %get-tuple-element.41, f32[6,16,1,16,16]{4,3,2,0,1:T(8,128)} %get-tuple-element.40, f32[6,16,15,16,16]{4,3,2,0,1:T(8,128)} %get-tuple-element.28, ...), kind=kLoop, calls=%fused_computation.2 | loop fusion | flops 6684672 | bytes 13074432 | tf_op jit(solution)/shard_map/sub | solution.py:103
  177.1 10.5 %reshape.114 = f32[6,16,4096]{2,0,1:T(8,128)} reshape(f32[6,16,16,16,16]{4,3,2,0,1:T(8,128)} %fusion) | data formatting | bytes 3145728 | tf_op jit(solution)/shard_map/reshape | solution.py:104
  187.6 4.7 fusion.14
  192.3 80.0 %psum.14 = f32[32,16]{0,1:T(8,128)S(1)} all-reduce(f32[32,16]{0,1:T(8,128)S(1)} %fusion.14), channel_id=1, replica_groups=mesh['px'=32,'py'=8] {'px','py'}, use_global_device_ids=true, to_apply=%region_0.0 | all-reduce | flops 512 | bytes 4096 | tf_op jit(solution)/shard_map/psum | solution.py:155
  272.4 4.1 fusion.6
  277.6 4.0 fusion.7
  281.6 5.7 convolution_bitcast_fusion.1
  287.3 9.7 %copy.50 = f32[6,48,32,128]{1,0,3,2:T(8,128)} copy(f32[6,48,32,128]{3,2,1,0:T(8,128)} %convolution_bitcast_fusion.1) | data formatting | bytes 9437184 | tf_op jit(solution)/shard_map/reshape | solution.py:47
  297.0 21.6 %gather_fusion = f32[2048,6,48]{2,1,0:T(8,128)} fusion(f32[6,48,4096]{1,0,2:T(8,128)} %bitcast.140, s32[2048]{0:T(1024)S(1)} %copy-done.10), kind=kCustom, calls=%fused_computation | custom fusion | bytes 4726784 | tf_op jit(solution)/shard_map/jit(_take)/gather | solution.py:158
  318.6 13.2 %multiply_reduce_fusion = f32[2048,48]{1,0:T(8,128)S(1)} fusion(f32[2048,6,48]{2,1,0:T(8,128)} %gather_fusion, f32[2048,6]{1,0:T(8,128)S(1)} %copy-done.7, pred[2048]{0:T(1024)(128)(4,1)S(1)} %copy-done.15), kind=kLoop, calls=%fused_computation.12 | loop fusion | flops 1671168 | bytes 2803712
  333.0 248.0 %all-reduce.7.cloned.1.call-done = f32[48,2048]{1,0:T(8,128)} async-done(((f32[48,2048]{1,0:T(8,128)}), f32[48,2048]{1,0:T(8,128)}) %all-reduce.7.cloned.1.call-update) | async-done | bytes 393232 | tf_op jit(solution)/shard_map/psum | solution.py:164
  (115 shorter events, 60.2 us)
Async XLA Ops:
  7.2 576.6 %copy-start = (f32[32,16]{0,1:T(8,128)S(1)}, f32[32,16]{0,1:T(8,128)}, u32[]{:S(2)}) copy-start(f32[32,16]{0,1:T(8,128)} %param.14) | copy-start | bytes 6148
  7.2 4.3 copy-start.9
  7.2 573.8 %all-reduce.7.cloned.1.call-start = ((), (), s32[]{:S(2)}) async-start(), calls=%async_computation | async-start | bytes 786432 | tf_op jit(solution)/shard_map/psum | solution.py:164
  9.1 104.6 %copy-start.12 = (f32[6]{0:T(128)}, f32[6]{0:T(128)S(1)}, u32[]{:S(2)}) copy-start(f32[6]{0:T(128)S(1)} %compare_convert_fusion) | copy-start | bytes 76
  23.7 92.0 %collective-permute-start.1 = (f32[1,17,256]{2,0,1:T(1,128)S(1)}, f32[1,17,256]{2,0,1:T(1,128)S(1)}, u32[]{:S(2)}, u32[]{:S(2)}) collective-permute-start(f32[1,17,256]{2,0,1:T(1,128)S(1)} %stack_reshape_squeeze.7), channel_id=1, source_target_pairs={{8,0},{16,8},{24,16},{32,24},{40,32},{48,40},{56,48},{64,56},{72,6... | collective-permute-start | bytes 52232 | tf_op jit(solution)/shard_map/ppermute | solution.py:23
  34.3 81.5 %collective-permute-start = (f32[1,17,256]{2,0,1:T(1,128)S(1)}, f32[1,17,256]{2,0,1:T(1,128)}, u32[]{:S(2)}, u32[]{:S(2)}) collective-permute-start(f32[1,17,256]{2,0,1:T(1,128)S(1)} %copy.46), channel_id=1, source_target_pairs={{0,8},{8,16},{16,24},{24,32},{32,40},{40,48},{48,56},{56,64},{64,7... | collective-permute-start | bytes 52232 | tf_op jit(solution)/shard_map/ppermute | solution.py:20
  52.5 76.8 %collective-permute-start.2 = (f32[1,6,17,256]{3,0,2,1:T(1,128)}, f32[1,6,17,256]{3,0,2,1:T(1,128)}, u32[]{:S(2)}, u32[]{:S(2)}) collective-permute-start(f32[1,6,17,256]{3,0,2,1:T(1,128)} %copy.47), channel_id=1, source_target_pairs={{0,1},{1,2},{2,3},{3,4},{4,5},{5,6},{6,7},{8,9},{9,10},{10,11},{11... | collective-permute-start | bytes 313352 | tf_op jit(solution)/shard_map/ppermute | solution.py:20
  58.6 21.2 %slice-start = ((s8[13369344]{0:T(1024)(128)(4,1)}), s8[4194304]{0:T(1024)(128)(4,1)S(1)}, s32[]{:S(2)}) async-start(s8[13369344]{0:T(1024)(128)(4,1)} %bitcast.138), calls=%async_computation.1 | async-start | bytes 8388608
  59.3 20.5 %slice-start.1 = ((s8[13369344]{0:T(1024)(128)(4,1)}), s8[4194304]{0:T(1024)(128)(4,1)S(1)}, s32[]{:S(2)}) async-start(s8[13369344]{0:T(1024)(128)(4,1)} %bitcast.138), calls=%async_computation.2 | async-start | bytes 8388608
  59.3 20.5 %slice-start.2 = ((s8[13369344]{0:T(1024)(128)(4,1)}), s8[4194304]{0:T(1024)(128)(4,1)S(1)}, s32[]{:S(2)}) async-start(s8[13369344]{0:T(1024)(128)(4,1)} %bitcast.138), calls=%async_computation.3 | async-start | bytes 8388608
  59.3 20.5 %slice-start.3 = ((s8[13369344]{0:T(1024)(128)(4,1)}), s8[786432]{0:T(1024)(128)(4,1)S(1)}, s32[]{:S(2)}) async-start(s8[13369344]{0:T(1024)(128)(4,1)} %bitcast.138), calls=%async_computation.4 | async-start | bytes 1572864
  59.3 64.3 %collective-permute-start.3 = (f32[1,6,17,256]{3,0,2,1:T(1,128)}, f32[1,6,17,256]{3,0,2,1:T(1,128)}, u32[]{:S(2)}, u32[]{:S(2)}) collective-permute-start(f32[1,6,17,256]{3,0,2,1:T(1,128)} %copy.48), channel_id=1, source_target_pairs={{1,0},{2,1},{3,2},{4,3},{5,4},{6,5},{7,6},{9,8},{10,9},{11,10},{12... | collective-permute-start | bytes 313352 | tf_op jit(solution)/shard_map/ppermute | solution.py:23
  100.1 5.1 copy-start.3
  101.5 5.2 copy-start.4
  102.8 5.4 copy-start.8
  102.8 5.5 copy-start.16
  116.7 5.6 copy-start.6
  177.1 10.5 %copy-start.13 = (f32[6]{0:T(128)S(1)}, f32[6]{0:T(128)}, u32[]{:S(2)}) copy-start(f32[6]{0:T(128)} %copy-done.12) | copy-start | bytes 76
  272.3 5.3 copy-start.1
  272.3 5.3 copy-start.2
  287.3 9.7 %copy-start.10 = (s32[2048]{0:T(1024)S(1)}, s32[2048]{0:T(1024)}, u32[]{:S(2)}) copy-start(s32[2048]{0:T(1024)} %get-tuple-element.33) | copy-start | bytes 24580
  297.0 21.6 %copy-start.7 = (f32[2048,6]{1,0:T(8,128)S(1)}, f32[2048,6]{1,0:T(8,128)}, u32[]{:S(2)}) copy-start(f32[2048,6]{1,0:T(8,128)} %copy.53) | copy-start | bytes 147460
  297.0 21.6 %copy-start.15 = (pred[2048]{0:T(1024)(128)(4,1)S(1)}, pred[2048]{0:T(1024)(128)(4,1)}, u32[]{:S(2)}) copy-start(pred[2048]{0:T(1024)(128)(4,1)} %compare_and_fusion) | copy-start | bytes 6148
  318.6 266.7 %copy-start.14 = (f32[16,16]{1,0:T(8,128)S(1)}, f32[16,16]{1,0:T(8,128)}, u32[]{:S(2)}) copy-start(f32[16,16]{1,0:T(8,128)} %param.13) | copy-start | bytes 3076
  (2 other events, 5.1 us)
Sparse Core Ops, SparseCore 0:
  333.1 247.8 all-reduce.6
where the time goes:
time: 612 us; the launch traced here: 604 us
  waiting for transfers between devices  248 us (41%)
  local copies, waits for them, and re-layouts  139 us (23%)
  other arithmetic  81.1 us (13%)
  blocking collectives  80 us (13%)
  matrix products  25.8 us (4%)
  between operations  16.2 us (3%)
  starting transfers between devices  14.1 us (2%)
    psum x1, waiting for transfers between devices, body(): sketch_whole = lax.psum(partial_value, ('px', 'py'))  248 us
    psum x1, blocking collectives, body(): proj_coef = lax.psum(local_gram, ('px', 'py')) / total_cells  80 us
    sub x1, other arithmetic, apply_operator(): summed = diag_sum * centre_vals - weighted  37.8 us
    slice x2, local copies, waits for them, and re-layouts, shift_pair(): lax.slice_in_dim(cube_vals, 1, PS, axis=axis_pos)  26.7 us
    gather x1, local copies, waits for them, and re-layouts, body(): picked = jnp.take(spread, sample_rows % CELLS, axis=2)  21.6 us
    slice x4, local copies, waits for them, and re-layouts, shift_pair(): lax.slice_in_dim(cube_vals, 0, PS - 1, axis=axis_pos)  13.8 us
    unnamed x3, other arithmetic  13.3 us
  transfers between devices with their start and end apart: 5, of which 1 were waited for; matrix products, arithmetic and copies ran while one was open for 15% of the time, Pallas kernels for 0%

commit v1 on v0

--- a/solution.py
+++ b/solution.py
@@ -161,7 +161,8 @@
     partial_value = jnp.einsum("sk,sjk->jk", weights, picked, precision=highest) * (
         1.0 / math.sqrt(total_cells)
     )
-    sketch_whole = lax.psum(partial_value, ("px", "py"))
+    _attach_fields = lambda field_in: lax.psum(lax.psum(field_in, "px"), "py")
+    sketch_whole = _attach_fields(partial_value)
     sketch_mine = lax.dynamic_slice_in_dim(sketch_whole, share_start, share_width, 1)
     normal_gram, normal_cross = normal_parts(
         sketch_whole, proj_coef, previous_coef, residual_factor

time: 612 us -> 572 us (0.935)
  waiting for transfers between devices: 248 us -> 207 us
    psum x1 -> x2, waiting for transfers between devices: 248 us -> 207 us  [body(): _attach_fields = lambda field_in: lax.psum(lax.psum(field_in, 'px'), 'py')]
  transfers between devices with their start and end apart: 5 -> 6, of which waited for: 1 -> 2; matrix products, arithmetic and copies ran while one was open for 15% -> 16% of each run, Pallas kernels for 0% -> 0%
where the time goes in v1:
time: 572 us; the launch traced here: 563 us
  waiting for transfers between devices  207 us (36%)
  local copies, waits for them, and re-layouts  139 us (24%)
  other arithmetic  81.1 us (14%)
  blocking collectives  80 us (14%)
  matrix products  25.8 us (5%)
  between operations  16.2 us (3%)
  starting transfers between devices  14.1 us (2%)
    psum x2, waiting for transfers between devices, body(): _attach_fields = lambda field_in: lax.psum(lax.psum(field_in, 'px'), 'py')  207 us
    psum x1, blocking collectives, body(): proj_coef = lax.psum(local_gram, ('px', 'py')) / total_cells  80 us
    sub x1, other arithmetic, apply_operator(): summed = diag_sum * centre_vals - weighted  37.8 us
    slice x2, local copies, waits for them, and re-layouts, shift_pair(): lax.slice_in_dim(cube_vals, 1, PS, axis=axis_pos)  26.7 us
    gather x1, local copies, waits for them, and re-layouts, body(): picked = jnp.take(spread, sample_rows % CELLS, axis=2)  21.6 us
    slice x4, local copies, waits for them, and re-layouts, shift_pair(): lax.slice_in_dim(cube_vals, 0, PS - 1, axis=axis_pos)  13.8 us
    unnamed x3, other arithmetic  13.3 us
  transfers between devices with their start and end apart: 6, of which 2 were waited for; matrix products, arithmetic and copies ran while one was open for 16% of the time, Pallas kernels for 0%

profile of v1, /device:TPU:1, one launch (start us, length us, event | category | flops | bytes accessed | tf_op | source)
XLA Modules:
  0.0 562.5 jit_solution(17391844290049469332)
XLA Ops:
  14.0 8.6 %reshape.92 = f32[6,17,16,16,16]{4,3,2,0,1:T(8,128)} reshape(f32[6,17,4096]{2,0,1:T(8,128)} %copy.21) | data formatting | bytes 3342336 | tf_op jit(solution)/shard_map/reshape | solution.py:69
  26.3 3.2 constant_dynamic-slice_fusion.1
  29.5 3.9 copy.22
  34.3 5.2 collective-permute-start
  39.5 10.8 %slice_reduce_fusion = (f32[6,17,16,16]{3,2,0,1:T(8,128)}, f32[6,17,16,16]{3,2,0,1:T(8,128)}) fusion(f32[6,17,16,16,16]{4,3,2,0,1:T(8,128)} %reshape.92), kind=kLoop, calls=%fused_computation.34 | loop fusion | bytes 417792 | tf_op jit(solution)/shard_map/slice | solution.py:74
  52.5 4.6 collective-permute-start.2
  62.4 17.5 %fusion.102 = (f32[6,16,15,16,16]{4,3,2,0,1:T(8,128)}, f32[6,16,15,16,16]{4,3,2,0,1:T(8,128)}) fusion(f32[6,17,16,16,16]{4,3,2,0,1:T(8,128)} %reshape.92), kind=kLoop, calls=%fused_computation.173 | loop fusion | bytes 5898240 | tf_op jit(solution)/shard_map/slice | solution.py:59
  81.1 9.2 %fusion.101 = (f32[6,16,16,15,16]{4,3,2,0,1:T(8,128)}, f32[6,16,16,15,16]{4,3,2,0,1:T(8,128)}) fusion(f32[6,17,16,16,16]{4,3,2,0,1:T(8,128)S(1)} %bitcast.139), kind=kLoop, calls=%fused_computation.172 | loop fusion | bytes 5898240 | tf_op jit(solution)/shard_map/slice | solution.py:59
  90.3 9.8 %fusion.100 = (f32[6,16,16,16,15]{4,3,2,0,1:T(8,128)}, f32[6,16,16,16,15]{4,3,2,0,1:T(8,128)}) fusion(f32[6,17,16,16,16]{4,3,2,0,1:T(8,128)S(1)} %bitcast.139), kind=kLoop, calls=%fused_computation.171 | loop fusion | bytes 5898240 | tf_op jit(solution)/shard_map/slice | solution.py:54
  109.1 4.0 bitcast_multiply_fusion.1
  118.9 3.5 fusion.30
  134.3 5.0 add_bitcast_fusion
  139.3 37.8 %fusion = f32[6,16,16,16,16]{4,3,2,0,1:T(8,128)} fusion(f32[6,17,16,16,16]{4,3,2,0,1:T(8,128)} %reshape.92, f32[6,16,15,16,16]{4,3,2,0,1:T(8,128)} %get-tuple-element.29, f32[6,16,1,16,16]{4,3,2,0,1:T(8,128)} %get-tuple-element.41, f32[6,16,1,16,16]{4,3,2,0,1:T(8,128)} %get-tuple-element.40, f32[6,16,15,16,16]{4,3,2,0,1:T(8,128)} %get-tuple-element.28, ...), kind=kLoop, calls=%fused_computation.2 | loop fusion | flops 6684672 | bytes 13074432 | tf_op jit(solution)/shard_map/sub | solution.py:103
  177.1 10.5 %reshape.114 = f32[6,16,4096]{2,0,1:T(8,128)} reshape(f32[6,16,16,16,16]{4,3,2,0,1:T(8,128)} %fusion) | data formatting | bytes 3145728 | tf_op jit(solution)/shard_map/reshape | solution.py:104
  187.6 4.7 fusion.14
  192.3 80.0 %psum.21 = f32[32,16]{0,1:T(8,128)S(1)} all-reduce(f32[32,16]{0,1:T(8,128)S(1)} %fusion.14), channel_id=1, replica_groups=mesh['px'=32,'py'=8] {'px','py'}, use_global_device_ids=true, to_apply=%region_0.0 | all-reduce | flops 512 | bytes 4096 | tf_op jit(solution)/shard_map/psum | solution.py:155
  272.4 4.1 fusion.6
  277.6 4.0 fusion.7
  281.7 5.7 %convolution_bitcast_fusion.1 = f32[6,48,32,128]{3,2,1,0:T(8,128)} fusion(f32[6,48,32,128]{3,2,1,0:T(8,128)S(1)} %fusion.7), kind=kOutput, calls=%fused_computation.25 | convolution fusion | flops 453000192 | bytes 9437184 | tf_op jit(solution)/shard_map/ca,sjad->sjcd/dot_general | solution.py:46
  287.3 9.7 %copy.50 = f32[6,48,32,128]{1,0,3,2:T(8,128)} copy(f32[6,48,32,128]{3,2,1,0:T(8,128)} %convolution_bitcast_fusion.1) | data formatting | bytes 9437184 | tf_op jit(solution)/shard_map/reshape | solution.py:47
  297.0 21.6 %gather_fusion = f32[2048,6,48]{2,1,0:T(8,128)} fusion(f32[6,48,4096]{1,0,2:T(8,128)} %bitcast.140, s32[2048]{0:T(1024)S(1)} %copy-done.10), kind=kCustom, calls=%fused_computation | custom fusion | bytes 4726784 | tf_op jit(solution)/shard_map/jit(_take)/gather | solution.py:158
  318.7 13.2 %multiply_reduce_fusion = f32[2048,48]{1,0:T(8,128)S(1)} fusion(f32[2048,6,48]{2,1,0:T(8,128)} %gather_fusion, f32[2048,6]{1,0:T(8,128)S(1)} %copy-done.7, pred[2048]{0:T(1024)(128)(4,1)S(1)} %copy-done.15), kind=kLoop, calls=%fused_computation.12 | loop fusion | flops 1671168 | bytes 2803712
  333.1 138.6 %all-reduce.8.cloned.1.call-done = f32[48,2048]{1,0:T(8,128)} async-done(((f32[48,2048]{1,0:T(8,128)}), f32[48,2048]{1,0:T(8,128)}) %all-reduce.8.cloned.1.call-update) | async-done | bytes 393232 | tf_op jit(solution)/shard_map/psum | solution.py:164
  471.7 68.0 %all-reduce.10.cloned.1.call-done = f32[48,2048]{1,0:T(8,128)} async-done(((f32[48,2048]{1,0:T(8,128)}), f32[48,2048]{1,0:T(8,128)}) %all-reduce.10.cloned.1.call-update) | async-done | bytes 393232 | tf_op jit(solution)/shard_map/psum | solution.py:164
  (118 shorter events, 63.2 us)
Async XLA Ops:
  7.2 535.2 %copy-start = (f32[32,16]{0,1:T(8,128)S(1)}, f32[32,16]{0,1:T(8,128)}, u32[]{:S(2)}) copy-start(f32[32,16]{0,1:T(8,128)} %param.14) | copy-start | bytes 6148
  7.2 464.5 %all-reduce.8.cloned.1.call-start = ((), (), s32[]{:S(2)}) async-start(), calls=%async_computation | async-start | bytes 786432 | tf_op jit(solution)/shard_map/psum | solution.py:164
  9.1 104.6 %copy-start.12 = (f32[6]{0:T(128)}, f32[6]{0:T(128)S(1)}, u32[]{:S(2)}) copy-start(f32[6]{0:T(128)S(1)} %compare_convert_fusion) | copy-start | bytes 76
  23.7 92.0 %collective-permute-start.1 = (f32[1,17,256]{2,0,1:T(1,128)S(1)}, f32[1,17,256]{2,0,1:T(1,128)S(1)}, u32[]{:S(2)}, u32[]{:S(2)}) collective-permute-start(f32[1,17,256]{2,0,1:T(1,128)S(1)} %stack_reshape_squeeze.7), channel_id=1, source_target_pairs={{8,0},{16,8},{24,16},{32,24},{40,32},{48,40},{56,48},{64,56},{72,6... | collective-permute-start | bytes 52232 | tf_op jit(solution)/shard_map/ppermute | solution.py:23
  34.3 81.5 %collective-permute-start = (f32[1,17,256]{2,0,1:T(1,128)S(1)}, f32[1,17,256]{2,0,1:T(1,128)}, u32[]{:S(2)}, u32[]{:S(2)}) collective-permute-start(f32[1,17,256]{2,0,1:T(1,128)S(1)} %copy.46), channel_id=1, source_target_pairs={{0,8},{8,16},{16,24},{24,32},{32,40},{40,48},{48,56},{56,64},{64,7... | collective-permute-start | bytes 52232 | tf_op jit(solution)/shard_map/ppermute | solution.py:20
  52.5 76.8 %collective-permute-start.2 = (f32[1,6,17,256]{3,0,2,1:T(1,128)}, f32[1,6,17,256]{3,0,2,1:T(1,128)}, u32[]{:S(2)}, u32[]{:S(2)}) collective-permute-start(f32[1,6,17,256]{3,0,2,1:T(1,128)} %copy.47), channel_id=1, source_target_pairs={{0,1},{1,2},{2,3},{3,4},{4,5},{5,6},{6,7},{8,9},{9,10},{10,11},{11... | collective-permute-start | bytes 313352 | tf_op jit(solution)/shard_map/ppermute | solution.py:20
  58.6 21.2 %slice-start = ((s8[13369344]{0:T(1024)(128)(4,1)}), s8[4194304]{0:T(1024)(128)(4,1)S(1)}, s32[]{:S(2)}) async-start(s8[13369344]{0:T(1024)(128)(4,1)} %bitcast.138), calls=%async_computation.2 | async-start | bytes 8388608
  59.3 20.5 %slice-start.1 = ((s8[13369344]{0:T(1024)(128)(4,1)}), s8[4194304]{0:T(1024)(128)(4,1)S(1)}, s32[]{:S(2)}) async-start(s8[13369344]{0:T(1024)(128)(4,1)} %bitcast.138), calls=%async_computation.3 | async-start | bytes 8388608
  59.3 20.5 %slice-start.2 = ((s8[13369344]{0:T(1024)(128)(4,1)}), s8[4194304]{0:T(1024)(128)(4,1)S(1)}, s32[]{:S(2)}) async-start(s8[13369344]{0:T(1024)(128)(4,1)} %bitcast.138), calls=%async_computation.4 | async-start | bytes 8388608
  59.3 20.5 %slice-start.3 = ((s8[13369344]{0:T(1024)(128)(4,1)}), s8[786432]{0:T(1024)(128)(4,1)S(1)}, s32[]{:S(2)}) async-start(s8[13369344]{0:T(1024)(128)(4,1)} %bitcast.138), calls=%async_computation.5 | async-start | bytes 1572864
  59.3 64.3 %collective-permute-start.3 = (f32[1,6,17,256]{3,0,2,1:T(1,128)}, f32[1,6,17,256]{3,0,2,1:T(1,128)}, u32[]{:S(2)}, u32[]{:S(2)}) collective-permute-start(f32[1,6,17,256]{3,0,2,1:T(1,128)} %copy.48), channel_id=1, source_target_pairs={{1,0},{2,1},{3,2},{4,3},{5,4},{6,5},{7,6},{9,8},{10,9},{11,10},{12... | collective-permute-start | bytes 313352 | tf_op jit(solution)/shard_map/ppermute | solution.py:23
  100.1 5.1 copy-start.3
  101.5 5.2 copy-start.4
  102.8 5.4 copy-start.8
  102.8 5.5 copy-start.16
  116.7 5.6 %copy-start.6 = (f32[5,17,16,16]{3,2,0,1:T(8,128)S(1)}, f32[5,17,16,16]{3,2,0,1:T(8,128)}, u32[]{:S(2)}) copy-start(f32[5,17,16,16]{3,2,0,1:T(8,128)} %get-tuple-element.31) | copy-start | bytes 261124
  177.1 10.5 %copy-start.13 = (f32[6]{0:T(128)S(1)}, f32[6]{0:T(128)}, u32[]{:S(2)}) copy-start(f32[6]{0:T(128)} %copy-done.12) | copy-start | bytes 76
  272.4 5.3 copy-start.1
  272.4 5.3 copy-start.2
  287.3 9.7 %copy-start.10 = (s32[2048]{0:T(1024)S(1)}, s32[2048]{0:T(1024)}, u32[]{:S(2)}) copy-start(s32[2048]{0:T(1024)} %get-tuple-element.33) | copy-start | bytes 24580
  297.0 21.6 %copy-start.7 = (f32[2048,6]{1,0:T(8,128)S(1)}, f32[2048,6]{1,0:T(8,128)}, u32[]{:S(2)}) copy-start(f32[2048,6]{1,0:T(8,128)} %copy.53) | copy-start | bytes 147460
  297.0 21.6 %copy-start.15 = (pred[2048]{0:T(1024)(128)(4,1)S(1)}, pred[2048]{0:T(1024)(128)(4,1)}, u32[]{:S(2)}) copy-start(pred[2048]{0:T(1024)(128)(4,1)} %compare_and_fusion) | copy-start | bytes 6148
  318.6 225.4 %copy-start.14 = (f32[16,16]{1,0:T(8,128)S(1)}, f32[16,16]{1,0:T(8,128)}, u32[]{:S(2)}) copy-start(f32[16,16]{1,0:T(8,128)} %param.13) | copy-start | bytes 3076
  333.0 206.7 %all-reduce.10.cloned.1.call-start = ((), (), s32[]{:S(2)}) async-start(), calls=%async_computation.1 | async-start | bytes 786432 | tf_op jit(solution)/shard_map/psum | solution.py:164
  (3 other events, 9.3 us)
Sparse Core Ops, SparseCore 0:
  333.1 138.5 all-reduce.7
  474.0 65.6 all-reduce.9
